TPU v7x, 32 devices: a whole 2x2x4 slice. The times are simulated.
32 devices in a mesh: layer: 8 (over z, x), row: 4 (over y, core).
Axes of the slice: x: 2, y: 2, z: 4, core: 2. Of those that a mesh axis runs over, the one named last changes fastest.
Arguments:
- leaf_rhs: bfloat16 [32768, 512], P(('layer', 'row')), may hold values from -3 to 3
- leaf_inv: bfloat16 [256, 128, 128], P(('layer', 'row')), may hold values from -1 to 1.25, as said below
- coupling: bfloat16 [32768, 3, 256], P(('layer', 'row')), may hold values from -0.09375 to 0.09375
- pattern: int32 [256, 3], P(('layer', 'row')), may hold values 0 or 1
- anc_rhs: float32 [8, 3, 1024, 512], P('layer', None, 'row'), may hold values from -2 to 2
- anc_blocks: bfloat16 [8, 6, 1024, 1024], P('layer', None, 'row'), may hold values from -1 to 1.25, as said below
Outputs:
- x_leaf: float32 [32768, 512], P(('layer', 'row'))
- x_anc: float32 [8, 3, 1024, 512], P('layer', None, 'row')
Inputs may be any that keep to these rules, and one draw needn't show every extreme that they name: `leaf_inv`: each block is lower triangular with a positive diagonal. For every level t and block index k of blk(s, t), the copies anc_blocks[l, k] are equal for all layers l of one group of 2 ** (t + 1) layers; the blocks blk(t, t) are lower triangular with a positive diagonal.
All inputs are finite; a program needn't handle non-finite values. No bound on the sum of `pattern` on one device may be relied on, other than what follows from the above.
Results may differ from a plain program's by a relative error of at most 0.009.
Values may be sent and summed in bfloat16 or wider, within the bound.
A program may use at most 64 MiB of HBM per device.

v0:
```python
import jax
import jax.numpy as jnp
from jax import lax
from jax.sharding import PartitionSpec as P


def partner(value, axis, bit):
    mask = 2**bit
    pairs = [(source, source ^ mask) for source in range(lax.axis_size(axis))]
    return lax.ppermute(value, axis, pairs)


def block_start(tree_level, level_total):
    return tree_level * level_total - tree_level * (tree_level - 1) // 2


def body(leaf_rhs, leaf_inv, coupling, pattern, anc_rhs, anc_blocks):
    levels_here = anc_rhs.shape[1]
    supers = leaf_inv.shape[0]
    block_width = leaf_inv.shape[1]
    num_sides = leaf_rhs.shape[1]
    sep_rows = anc_rhs.shape[2]
    leaf_rows = supers * block_width
    leaf_y = jnp.einsum(
        "kab,kbr->kar",
        leaf_inv,
        leaf_rhs.reshape(supers, block_width, num_sides),
        preferred_element_type=jnp.float32,
    )
    leaf_yb = leaf_y.astype(jnp.bfloat16).reshape(leaf_rows, num_sides)
    masked = (
        coupling.reshape(supers, block_width, levels_here, sep_rows)
        * pattern.astype(jnp.bfloat16)[:, None, :, None]
    )
    masked = masked.reshape(leaf_rows, levels_here * sep_rows)
    leaf_terms = lax.dot_general(
        masked, leaf_yb, (((0,), (0,)), ((), ())), preferred_element_type=jnp.float32
    )
    pending = anc_rhs[0] - leaf_terms.reshape(levels_here, sep_rows, num_sides)
    solved = []
    for tree_level in range(levels_here):
        first_block = block_start(tree_level, levels_here)
        block_count = levels_here - tree_level
        stacked = anc_blocks[0, first_block : first_block + block_count].reshape(
            block_count * sep_rows, -1
        )
        upper_sums = pending[tree_level:]
        upper_sums = upper_sums + partner(upper_sums, "layer", tree_level)
        pending = pending.at[tree_level:].set(upper_sums)
        level_total = upper_sums[0]
        level_z = level_total.astype(jnp.bfloat16)

        def accumulate(running, shard_piece, first_row, stacked=stacked):
            return jnp.dot(stacked, shard_piece, preferred_element_type=jnp.float32)

        product = accumulate(
            jnp.zeros((block_count * sep_rows, num_sides), jnp.float32),
            lax.all_gather(level_z, "row", axis=0, tiled=True),
            jnp.int32(0),
        )
        solved.append(product[:sep_rows].astype(jnp.bfloat16))
        if block_count > 1:
            later_terms = product[sep_rows:].reshape(block_count - 1, sep_rows, num_sides)
            pending = pending.at[tree_level + 1 :].add(-later_terms)
    answers = [None] * levels_here
    for tree_level in reversed(range(levels_here)):
        first_block = block_start(tree_level, levels_here)
        block_count = levels_here - tree_level
        stacked_vals = jnp.stack(
            [solved[tree_level]]
            + [-answers[above].astype(jnp.bfloat16) for above in range(tree_level + 1, levels_here)]
        )
        factor = anc_blocks[0, first_block : first_block + block_count]

        def transposed(first_row, row_count, factor=factor, stacked_vals=stacked_vals):
            return lax.dot_general(
                factor,
                stacked_vals,
                (((0, 1), (0, 1)), ((), ())),
                preferred_element_type=jnp.float32,
            )

        answers[tree_level] = lax.psum_scatter(
            transposed(jnp.int32(0), sep_rows * lax.axis_size("row")),
            "row",
            scatter_dimension=0,
            tiled=True,
        )
    anc_out = jnp.stack(answers)
    solved_bf = anc_out.astype(jnp.bfloat16).reshape(levels_here * sep_rows, num_sides)
    back_terms = jnp.dot(masked, solved_bf, preferred_element_type=jnp.float32)
    leaf_vb = (leaf_y.reshape(leaf_rows, num_sides) - back_terms).astype(jnp.bfloat16)
    x_leaf = jnp.einsum(
        "kba,kbr->kar",
        leaf_inv,
        leaf_vb.reshape(supers, block_width, num_sides),
        preferred_element_type=jnp.float32,
    )
    return (x_leaf.reshape(leaf_rows, num_sides), anc_out[None])


def solution(mesh):
    placed = (
        P(("layer", "row"), None),
        P(("layer", "row"), None, None),
        P(("layer", "row"), None, None),
        P(("layer", "row"), None),
        P("layer", None, "row", None),
        P("layer", None, "row", None),
    )
    return jax.shard_map(
        body,
        mesh=mesh,
        in_specs=placed,
        out_specs=(P(("layer", "row"), None), P("layer", None, "row", None)),
        check_vma=False,
    )
```

profile of v0, /device:TPU:0, one launch (start us, length us, event | category | flops | bytes accessed | tf_op | source)
XLA Modules:
  0.0 284.5 jit_solution(10463308634355087739)
XLA Ops:
  8.0 1.7 copy.16
  10.9 1.7 fusion.33
  13.7 3.0 %collective-permute-start = (f32[3,256,512]{2,1,0:T(8,128)S(1)}, f32[3,256,512]{2,1,0:T(8,128)S(1)}, u32[]{:S(2)}, u32[]{:S(2)}) collective-permute-start(f32[3,256,512]{2,1,0:T(8,128)S(1)} %bitcast_subtract_fusion.1), channel_id=1, source_target_pairs={{0,4},{4,0},{8,12},{12,8},{16,20},{20,16},{24,28},{28,24},{1,5},{5... | collective-permute-start | bytes 4718600 | tf_op jit(solution)/shard_map/ppermute | solution.py:10
  16.7 34.4 %collective-permute-done = f32[3,256,512]{2,1,0:T(8,128)S(1)} collective-permute-done((f32[3,256,512]{2,1,0:T(8,128)S(1)}, f32[3,256,512]{2,1,0:T(8,128)S(1)}, u32[]{:S(2)}, u32[]{:S(2)}) %collective-permute-start) | collective-permute-done | bytes 1572896 | tf_op jit(solution)/shard_map/ppermute | solution.py:10
  52.3 2.7 slice.127
  54.9 15.6 %all-gather.7.cloned.1.call-done = bf16[1,1024,512]{2,1,0:T(8,128)(2,1)} async-done(((bf16[1,256,512]{2,1,0:T(8,128)(2,1)}), bf16[1,1024,512]{2,1,0:T(8,128)(2,1)}) %all-gather.7.cloned.1.call-update) | async-done | bytes 1048592 | tf_op jit(solution)/shard_map/all_gather | solution.py:58
  70.6 2.7 convolution_bitcast_fusion.3
  74.4 1.5 collective-permute-start.1
  75.9 23.8 %collective-permute-done.1 = f32[2,256,512]{2,1,0:T(8,128)S(1)} collective-permute-done((f32[2,256,512]{2,1,0:T(8,128)S(1)}, f32[2,256,512]{2,1,0:T(8,128)S(1)}, u32[]{:S(2)}, u32[]{:S(2)}) %collective-permute-start.1) | collective-permute-done | bytes 1048608 | tf_op jit(solution)/shard_map/ppermute | solution.py:10
  100.7 16.8 %all-gather.9.cloned.1.call-done = bf16[1,1024,512]{2,1,0:T(8,128)(2,1)} async-done(((bf16[1,256,512]{2,1,0:T(8,128)(2,1)}), bf16[1,1024,512]{2,1,0:T(8,128)(2,1)}) %all-gather.9.cloned.1.call-update) | async-done | bytes 1048592 | tf_op jit(solution)/shard_map/all_gather | solution.py:58
  117.5 1.9 convolution_bitcast_fusion.4
  119.6 2.5 collective-permute-start.2
  122.0 23.8 %collective-permute-done.2 = f32[1,256,512]{2,1,0:T(8,128)S(1)} collective-permute-done((f32[1,256,512]{2,1,0:T(8,128)S(1)}, f32[1,256,512]{2,1,0:T(8,128)S(1)}, u32[]{:S(2)}, u32[]{:S(2)}) %collective-permute-start.2) | collective-permute-done | bytes 524320 | tf_op jit(solution)/shard_map/ppermute | solution.py:10
  146.7 16.8 %all-gather.11.cloned.1.call-done = bf16[1,1024,512]{2,1,0:T(8,128)(2,1)} async-done(((bf16[1,256,512]{2,1,0:T(8,128)(2,1)}), bf16[1,1024,512]{2,1,0:T(8,128)(2,1)}) %all-gather.11.cloned.1.call-update) | async-done | bytes 1048592 | tf_op jit(solution)/shard_map/all_gather | solution.py:58
  163.5 4.2 %convolution_bitcast_fusion.1 = f32[1024,512]{1,0:T(8,128)} fusion(bf16[1,1024,512]{2,1,0:T(8,128)(2,1)} %all-gather.11.cloned.1.call-done, bf16[1,6,256,1024]{3,2,1,0:T(8,128)(2,1)} %param.21), kind=kOutput, calls=%fused_computation.3 | convolution fusion | flops 537001984 | bytes 4194304 | tf_op jit(solution)/shard_map/dot_general | solution.py:76
  168.8 30.2 %reduce-scatter.4.cloned.1.call-done = f32[256,512]{1,0:T(8,128)} async-done(((f32[1024,512]{1,0:T(8,128)}), f32[256,512]{1,0:T(8,128)}) %reduce-scatter.4.cloned.1.call-update) | async-done | bytes 524304 | tf_op jit(solution)/shard_map/reduce_scatter | solution.py:83
  200.1 3.3 %convolution_bitcast_fusion = f32[1024,512]{1,0:T(8,128)} fusion(bf16[1,256,512]{2,1,0:T(8,128)(2,1)S(1)} %negate_bitcast_fusion.1, bf16[1,256,512]{2,1,0:T(8,128)(2,1)S(1)} %fusion.27, bf16[1,6,256,1024]{3,2,1,0:T(8,128)(2,1)} %param.21), kind=kOutput, calls=%fused_computation.2 | convolution fusion | flops 537133056 | bytes 3670016 | tf_op jit(solution)/shard_map/dot_general | solution.py:76
  203.5 1.1 fusion.26
  204.5 30.2 %reduce-scatter.6.cloned.1.call-done = f32[256,512]{1,0:T(8,128)} async-done(((f32[1024,512]{1,0:T(8,128)}), f32[256,512]{1,0:T(8,128)}) %reduce-scatter.6.cloned.1.call-update) | async-done | bytes 524304 | tf_op jit(solution)/shard_map/reduce_scatter | solution.py:83
  235.8 3.8 %convolution_bitcast_fusion.2 = f32[1024,512]{1,0:T(8,128)} fusion(bf16[1,256,512]{2,1,0:T(8,128)(2,1)S(1)} %negate_bitcast_fusion.1, bf16[1,256,512]{2,1,0:T(8,128)(2,1)S(1)} %negate_bitcast_fusion, bf16[1,256,512]{2,1,0:T(8,128)(2,1)S(1)} %fusion.26, bf16[1,6,256,1024]{3,2,1,0:T(8,128)(2,1)} %param.21), kind=kOutput, calls=%fused_computation.4 | convolution fusion | flops 806092800 | bytes 4456448 | tf_op jit(solution)/shard_map/dot_general | solution.py:76
  239.7 31.2 %reduce-scatter.8.cloned.1.call-done = f32[256,512]{1,0:T(8,128)} async-done(((f32[1024,512]{1,0:T(8,128)}), f32[256,512]{1,0:T(8,128)}) %reduce-scatter.8.cloned.1.call-update) | async-done | bytes 524304 | tf_op jit(solution)/shard_map/reduce_scatter | solution.py:83
  270.9 2.5 fusion.3
  273.4 2.4 fusion
  275.9 1.8 fusion.34
  (49 shorter events, 10.7 us)
Async XLA Ops:
  7.2 3.2 %copy-start = (bf16[1024,512]{1,0:T(8,128)(2,1)S(1)}, bf16[1024,512]{1,0:T(8,128)(2,1)}, u32[]{:S(2)}) copy-start(bf16[1024,512]{1,0:T(8,128)(2,1)} %param.16) | copy-start | bytes 3145732
  7.2 63.4 %all-gather.7.cloned.1.call-start = ((), (), s32[]{:S(2)}) async-start(), calls=%async_computation.6 | async-start | bytes 1310720 | tf_op jit(solution)/shard_map/all_gather | solution.py:58
  10.0 1.0 copy-start.5
  10.9 1.7 copy-start.8
  13.7 37.4 %collective-permute-start = (f32[3,256,512]{2,1,0:T(8,128)S(1)}, f32[3,256,512]{2,1,0:T(8,128)S(1)}, u32[]{:S(2)}, u32[]{:S(2)}) collective-permute-start(f32[3,256,512]{2,1,0:T(8,128)S(1)} %bitcast_subtract_fusion.1), channel_id=1, source_target_pairs={{0,4},{4,0},{8,12},{12,8},{16,20},{20,16},{24,28},{28,24},{1,5},{5... | collective-permute-start | bytes 4718600 | tf_op jit(solution)/shard_map/ppermute | solution.py:10
  52.2 65.3 %all-gather.9.cloned.1.call-start = ((), (), s32[]{:S(2)}) async-start(), calls=%async_computation.7 | async-start | bytes 1310720 | tf_op jit(solution)/shard_map/all_gather | solution.py:58
  73.3 1.1 copy-start.4
  74.4 25.3 %collective-permute-start.1 = (f32[2,256,512]{2,1,0:T(8,128)S(1)}, f32[2,256,512]{2,1,0:T(8,128)S(1)}, u32[]{:S(2)}, u32[]{:S(2)}) collective-permute-start(f32[2,256,512]{2,1,0:T(8,128)S(1)} %slice_add_fusion), channel_id=1, source_target_pairs={{0,8},{4,12},{8,0},{12,4},{16,24},{20,28},{24,16},{28,20},{1,9},{5... | collective-permute-start | bytes 3145736 | tf_op jit(solution)/shard_map/ppermute | solution.py:10
  99.9 17.6 %slice-start = ((bf16[1,6,256,1024]{3,2,1,0:T(8,128)(2,1)}), bf16[1,2,256,1024]{3,2,1,0:T(8,128)(2,1)S(1)}, s32[]{:S(2)}) async-start(bf16[1,6,256,1024]{3,2,1,0:T(8,128)(2,1)} %param.21), calls=%async_computation.9 | async-start | bytes 2097152 | tf_op jit(solution)/shard_map/slice | solution.py:73
  100.7 62.8 %all-gather.11.cloned.1.call-start = ((), (), s32[]{:S(2)}) async-start(), calls=%async_computation.8 | async-start | bytes 1310720 | tf_op jit(solution)/shard_map/all_gather | solution.py:58
  119.5 26.4 %copy-start.6 = (f32[512,512]{1,0:T(8,128)}, f32[512,512]{1,0:T(8,128)S(1)}, u32[]{:S(2)}) copy-start(f32[512,512]{1,0:T(8,128)S(1)} %convolution_bitcast_fusion.4) | copy-start | bytes 3145732
  119.6 26.3 %collective-permute-start.2 = (f32[1,256,512]{2,1,0:T(8,128)S(1)}, f32[1,256,512]{2,1,0:T(8,128)S(1)}, u32[]{:S(2)}, u32[]{:S(2)}) collective-permute-start(f32[1,256,512]{2,1,0:T(8,128)S(1)} %fusion.18), channel_id=1, source_target_pairs={{0,16},{4,20},{8,24},{12,28},{16,0},{20,4},{24,8},{28,12},{1,17},{... | collective-permute-start | bytes 1572872 | tf_op jit(solution)/shard_map/ppermute | solution.py:10
  146.6 52.4 %reduce-scatter.4.cloned.1.call-start = ((), (), s32[]{:S(2)}) async-start(), calls=%async_computation.3 | async-start | bytes 2621440 | tf_op jit(solution)/shard_map/reduce_scatter | solution.py:83
  167.7 67.1 %reduce-scatter.6.cloned.1.call-start = ((), (), s32[]{:S(2)}) async-start(), calls=%async_computation.4 | async-start | bytes 2621440 | tf_op jit(solution)/shard_map/reduce_scatter | solution.py:83
  203.4 67.5 %reduce-scatter.8.cloned.1.call-start = ((), (), s32[]{:S(2)}) async-start(), calls=%async_computation.5 | async-start | bytes 2621440 | tf_op jit(solution)/shard_map/reduce_scatter | solution.py:83
  239.6 31.3 %copy-start.2 = (f32[256,512]{1,0:T(8,128)S(1)}, f32[256,512]{1,0:T(8,128)}, u32[]{:S(2)}) copy-start(f32[256,512]{1,0:T(8,128)} %reduce-scatter.4.cloned.1.call-done) | copy-start | bytes 1572868
  239.6 31.3 %copy-start.3 = (f32[256,512]{1,0:T(8,128)S(1)}, f32[256,512]{1,0:T(8,128)}, u32[]{:S(2)}) copy-start(f32[256,512]{1,0:T(8,128)} %reduce-scatter.6.cloned.1.call-done) | copy-start | bytes 1572868
  270.9 2.5 copy-start.1
  270.9 2.5 copy-start.7
Sparse Core Ops, SparseCore 0:
  52.3 18.1 all-gather.6
  100.8 16.6 all-gather.8
  146.8 16.6 all-gather.10
  167.8 31.1 reduce-scatter.3
  203.5 31.1 reduce-scatter.5
  239.7 31.1 reduce-scatter.7
where the time goes:
time: 285 us
  waiting for transfers between devices  223 us (78%)
  matrix products  22.9 us (8%)
  between operations  14.3 us (5%)
  local copies, waits for them, and re-layouts  9.83 us (3%)
  other arithmetic  7.43 us (3%)
  starting transfers between devices  7.23 us (3%)
    reduce_scatter x3, waiting for transfers between devices, body(): lax.psum_scatter(transposed(jnp.int32(0), sep_rows * lax.axis_size('row')...  91.6 us
    ppermute x3, waiting for transfers between devices, partner(): return lax.ppermute(value, axis, pairs)  82 us
    all_gather x3, waiting for transfers between devices, body(): lax.all_gather(level_z, 'row', axis=0, tiled=True)  49.2 us
    dot_general x3, matrix products, transposed(): lax.dot_general(factor, stacked_vals, (((0, 1), (0, 1)), ((), ())), prefe...  11.3 us
    ppermute x3, starting transfers between devices, partner(): return lax.ppermute(value, axis, pairs)  6.98 us
  transfers between devices with their start and end apart: 9, of which 9 were waited for; matrix products, arithmetic and copies ran while one was open for 2% of the time, Pallas kernels for 0%

commit v1 on v0

v1 whole, which is shorter than its diff:
```python
import functools

import jax
import jax.numpy as jnp
from jax import lax
from jax.experimental import pallas as pl
from jax.experimental.pallas import tpu as pltpu
from jax.sharding import PartitionSpec as P

MESH = pl.DeviceIdType.MESH
LANES = 128


def block_start(tree_level, level_total):
    return tree_level * level_total - tree_level * (tree_level - 1) // 2


def plan(levels, cols):
    widths, splits, width = [], [], cols
    for _ in range(levels):
        split = width % (2 * LANES) == 0
        width = width // 2 if split else width
        widths.append(width)
        splits.append(split)
    return widths, splits


def tdot(a, b):
    return lax.dot_general(a, b, (((0,), (0,)), ((), ())), preferred_element_type=jnp.float32)


def dot(a, b):
    return jnp.dot(a, b, preferred_element_type=jnp.float32)


class Copies:
    def __init__(self, send, recv):
        self.send, self.recv, self.count, self.all = send, recv, 0, []

    def start(self, src, dst, device):
        copy = pltpu.make_async_remote_copy(
            src_ref=src,
            dst_ref=dst,
            send_sem=self.send.at[self.count],
            recv_sem=self.recv.at[self.count],
            device_id=device,
            device_id_type=MESH,
        )
        copy.start()
        self.count += 1
        self.all.append(copy)
        return copy


def copies_needed(levels, n_row, splits):
    half = n_row // 2
    total = 0
    for t in range(levels):
        total += 2
        total += 1 + 2 * (half - 1)
        total += half + half - 1
        total += (levels - t) if splits[t] else 0
    return total


def separators(dims, share, anc, out, refs):
    levels, n_row, rows, cols = dims
    widths, splits = plan(levels, cols)
    half = n_row // 2
    tx, rx, pend, zs, acc, ps, pr, qs, qr, wide, send, recv = refs
    lay = lax.axis_index("layer")
    row = lax.axis_index("row")
    core = lax.rem(row, 2)
    yy = row // 2
    mate = {"row": yy * 2 + (1 - core)}
    bits = [lax.rem(lay // 2**t, 2) for t in range(levels)]
    across = [{"layer": lay + (1 - 2 * bits[t]) * 2**t} for t in range(levels)]

    barrier = pltpu.get_barrier_semaphore()
    for t in range(levels):
        pl.semaphore_signal(barrier, inc=1, device_id=across[t], device_id_type=MESH)
    for i in range(1, n_row):
        pl.semaphore_signal(
            barrier, inc=1, device_id={"row": lax.rem(row + i, n_row)}, device_id_type=MESH
        )
    pl.semaphore_wait(barrier, levels + n_row - 1)
    copies = Copies(send, recv)

    def piece(t, which):
        return pl.ds(pl.multiple_of(which * widths[t], LANES), widths[t])

    def offer(t, source):
        for s in range(t, levels):
            if splits[t]:
                value = source(s, piece(t, 1 - bits[t]))
            else:
                value = source(s, slice(None))
            tx[t][s - t] = value.astype(jnp.bfloat16)
            if s == t:
                first = copies.start(tx[t].at[pl.ds(0, 1)], rx[t].at[pl.ds(0, 1)], across[t])
        rest = None
        if levels - t > 1:
            later = pl.ds(1, levels - t - 1)
            rest = copies.start(tx[t].at[later], rx[t].at[later], across[t])
        return first, rest

    def source_share(s, part):
        return share[s, :, part]

    source = source_share
    flight = offer(0, source)
    later_work = None
    for t in range(levels):
        own = piece(t, bits[t]) if splits[t] else slice(None)
        if later_work is not None:
            later_work()
        flight[0].wait_recv()
        zs[t][row] = (source(t, own) + rx[t][0].astype(jnp.float32)).astype(jnp.bfloat16)
        gathers = []
        for i in range(1, half):
            other = lax.rem(yy + i, half) * 2 + core
            gathers.append(copies.start(zs[t].at[row], zs[t].at[row], {"row": other}))
        to_mate = copies.start(zs[t].at[row], zs[t].at[row], mate)
        if flight[1] is not None:
            flight[1].wait_recv()
        first_block = block_start(t, levels)
        above = levels - t - 1

        def sums_of(slot, t=t, first_block=first_block, above=above):
            column = pl.ds(pl.multiple_of(slot * rows, LANES), rows)
            return [dot(anc[first_block + 1 + k, :, column], zs[t][slot]) for k in range(above)]

        def add(old, new):
            return [a + b for a, b in zip(old, new)]

        total = sums_of(row)
        to_mate.wait_recv()
        total = add(total, sums_of(yy * 2 + 1 - core))
        passed = []
        for i in range(1, half):
            gathers[i - 1].wait_recv()
            origin = lax.rem(yy - i + half, half) * 2
            passed.append(copies.start(zs[t].at[origin + core], zs[t].at[origin + core], mate))
            total = add(total, sums_of(origin + core))
        for i in range(1, half):
            passed[i - 1].wait_recv()
            origin = lax.rem(yy - i + half, half) * 2
            total = add(total, sums_of(origin + 1 - core))
        for k in range(above):
            pend[t][k] = source(t + 1 + k, own) + rx[t][1 + k].astype(jnp.float32) - total[k]

        def source_pend(s, part, t=t):
            return pend[t][s - t - 1, :, part]

        source = source_pend
        if t + 1 < levels:
            flight = offer(t + 1, source)

        def later_work(t=t, first_block=first_block):
            z_all = zs[t][...].reshape(n_row * rows, widths[t])
            y_here = dot(anc[first_block], z_all).astype(jnp.bfloat16)
            for other in range(n_row):
                acc[t][other] = tdot(anc[first_block, :, other * rows : (other + 1) * rows], y_here)

    later_work()
    at = {}
    for t in reversed(range(levels)):
        first_block = block_start(t, levels)
        mine = piece(t, bits[t])
        widening = {}
        for s in range(t + 1, levels):
            if splits[t]:
                wider = wide[s][t]
                wider[:, mine] = at[s][...]
                widening[s] = copies.start(wider.at[:, mine], wider.at[:, mine], across[t])

        def part_of(dest, t=t, first_block=first_block):
            column = pl.ds(pl.multiple_of(dest * rows, LANES), rows)
            value = acc[t][dest]
            for s in range(t + 1, levels):
                value = value - tdot(anc[first_block + s - t, :, column], at[s][...])
            return value

        first_stage = []
        order = list(range(1, half)) + [0]
        for i in order:
            dest = lax.rem(yy + i, half) * 2 + 1 - core
            ps[t][i] = part_of(dest).astype(jnp.bfloat16)
            first_stage.append(copies.start(ps[t].at[i], pr[t].at[i], mate))
        second_stage = []
        for n, i in enumerate(order[:-1]):
            dest = lax.rem(yy + i, half) * 2 + core
            value = part_of(dest)
            first_stage[n].wait_recv()
            qs[t][i - 1] = (value + pr[t][i].astype(jnp.float32)).astype(jnp.bfloat16)
            second_stage.append(copies.start(qs[t].at[i - 1], qr[t].at[i - 1], {"row": dest}))
        value = part_of(row)
        first_stage[-1].wait_recv()
        value = value + pr[t][0].astype(jnp.float32)
        for n, i in enumerate(order[:-1]):
            second_stage[n].wait_recv()
            value = value + qr[t][i - 1].astype(jnp.float32)
        rounded = value.astype(jnp.bfloat16)
        wider = wide[t][t]
        if splits[t]:
            wider[:, mine] = rounded
            widening[t] = copies.start(wider.at[:, mine], wider.at[:, mine], across[t])
        else:
            wider[...] = rounded
        for s in range(t, levels):
            if splits[t]:
                widening[s].wait_recv()
                at[s] = wide[s][t]
            elif s == t:
                at[s] = wider
    for s in range(levels):
        out[s] = at[s][...]
    for copy in copies.all:
        copy.wait_send()


def kernel(dims, counts, share, anc, out, *scratch):
    refs, used = [], 0
    for count in counts:
        refs.append(scratch[used : used + count])
        used += count
    levels = dims[0]
    wide_flat = refs[-1]
    wide, used_wide = [], 0
    for s in range(levels):
        wide.append(wide_flat[used_wide : used_wide + s + 1])
        used_wide += s + 1
    send, recv = scratch[used:]
    separators(dims, share, anc, out, (*refs[:-1], wide, send, recv))


def solve_separators(share, anc):
    levels, rows, cols = share.shape
    n_row = lax.axis_size("row")
    half = n_row // 2
    widths, splits = plan(levels, cols)
    outer = [cols] + widths[:-1]
    span = range(levels)
    bf, f32 = jnp.bfloat16, jnp.float32
    groups = [
        [pltpu.VMEM((levels - t, rows, widths[t]), bf) for t in span],
        [pltpu.VMEM((levels - t, rows, widths[t]), bf) for t in span],
        [pltpu.VMEM((max(levels - t - 1, 1), rows, widths[t]), f32) for t in span],
        [pltpu.VMEM((n_row, rows, widths[t]), bf) for t in span],
        [pltpu.VMEM((n_row, rows, widths[t]), f32) for t in span],
        [pltpu.VMEM((half, rows, widths[t]), bf) for t in span],
        [pltpu.VMEM((half, rows, widths[t]), bf) for t in span],
        [pltpu.VMEM((max(half - 1, 1), rows, widths[t]), bf) for t in span],
        [pltpu.VMEM((max(half - 1, 1), rows, widths[t]), bf) for t in span],
        [pltpu.VMEM((rows, outer[t]), bf) for s in span for t in range(s + 1)],
    ]
    total = copies_needed(levels, n_row, splits)
    scratch = [ref for group in groups for ref in group]
    scratch += [pltpu.SemaphoreType.DMA((total,)), pltpu.SemaphoreType.DMA((total,))]
    return pl.pallas_call(
        functools.partial(kernel, (levels, n_row, rows, cols), [len(g) for g in groups]),
        out_shape=jax.ShapeDtypeStruct((levels, rows, cols), bf),
        in_specs=[pl.BlockSpec(memory_space=pltpu.VMEM)] * 2,
        out_specs=pl.BlockSpec(memory_space=pltpu.VMEM),
        scratch_shapes=scratch,
        compiler_params=pltpu.CompilerParams(collective_id=0, has_side_effects=True),
        name="separators",
    )(share, anc)


def body(leaf_rhs, leaf_inv, coupling, pattern, anc_rhs, anc_blocks):
    levels_here = anc_rhs.shape[1]
    supers = leaf_inv.shape[0]
    block_width = leaf_inv.shape[1]
    num_sides = leaf_rhs.shape[1]
    sep_rows = anc_rhs.shape[2]
    leaf_rows = supers * block_width
    leaf_y = jnp.einsum(
        "kab,kbr->kar",
        leaf_inv,
        leaf_rhs.reshape(supers, block_width, num_sides),
        preferred_element_type=jnp.float32,
    )
    leaf_yb = leaf_y.astype(jnp.bfloat16).reshape(leaf_rows, num_sides)
    masked = (
        coupling.reshape(supers, block_width, levels_here, sep_rows)
        * pattern.astype(jnp.bfloat16)[:, None, :, None]
    )
    masked = masked.reshape(leaf_rows, levels_here * sep_rows)
    leaf_terms = tdot(masked, leaf_yb)
    share = anc_rhs[0] - leaf_terms.reshape(levels_here, sep_rows, num_sides)
    solved = solve_separators(share, anc_blocks[0])
    solved_bf = solved.reshape(levels_here * sep_rows, num_sides)
    anc_out = solved.astype(jnp.float32)
    back_terms = dot(masked, solved_bf)
    leaf_vb = (leaf_y.reshape(leaf_rows, num_sides) - back_terms).astype(jnp.bfloat16)
    x_leaf = jnp.einsum(
        "kba,kbr->kar",
        leaf_inv,
        leaf_vb.reshape(supers, block_width, num_sides),
        preferred_element_type=jnp.float32,
    )
    return (x_leaf.reshape(leaf_rows, num_sides), anc_out[None])


def solution(mesh):
    placed = (
        P(("layer", "row"), None),
        P(("layer", "row"), None, None),
        P(("layer", "row"), None, None),
        P(("layer", "row"), None),
        P("layer", None, "row", None),
        P("layer", None, "row", None),
    )
    return jax.shard_map(
        body,
        mesh=mesh,
        in_specs=placed,
        out_specs=(P(("layer", "row"), None), P("layer", None, "row", None)),
        check_vma=False,
    )
```

time: 285 us -> 75.5 us (0.26)
  waiting for transfers between devices: 223 us -> 0 us
  Pallas kernels: 0 us -> 59.3 us
  matrix products: 22.9 us -> 7 us
  between operations: 14.3 us -> 0.71 us
  starting transfers between devices: 7.23 us -> 0 us
  local copies, waits for them, and re-layouts: 9.83 us -> 4.2 us
  other arithmetic: 7.43 us -> 3.78 us
    reduce_scatter x3 -> x0, waiting for transfers between devices: 91.6 us -> none  [body(): lax.psum_scatter(transposed(jnp.int32(0), sep_rows * lax.axis_size('row')...]
    ppermute x3 -> x0, waiting for transfers between devices: 82 us -> none  [partner(): return lax.ppermute(value, axis, pairs)]
    pallas_call x0 -> x1, Pallas kernels: none -> 59.3 us  [solve_separators(): pl.pallas_call(functools.partial(kernel, (levels, n_row, rows, cols), [le...]
    all_gather x3 -> x0, waiting for transfers between devices: 49.2 us -> none  [body(): lax.all_gather(level_z, 'row', axis=0, tiled=True)]
    dot_general x7 -> x2, matrix products: 19.3 us -> 4.78 us  [the longest x1 2.64 us: dot(): return jnp.dot(a, b, preferred_element_type=jnp.float32)]
    ppermute x3 -> x0, starting transfers between devices: 6.98 us -> none  [partner(): return lax.ppermute(value, axis, pairs)]
    slice x5 -> x0, local copies, waits for them, and re-layouts: 4.15 us -> none  [the longest x3 2.68 us: body(): factor = anc_blocks[0, first_block:first_block + block_count]]
  transfers between devices with their start and end apart: 9 -> 0, of which waited for: 9 -> 0; matrix products, arithmetic and copies ran while one was open for 2% -> 0% of each run, Pallas kernels for 0% -> 0%
where the time goes in v1:
time: 75.5 us; the launch traced here: 75 us
  Pallas kernels  59.3 us (79%)
  matrix products  7 us (9%)
  local copies, waits for them, and re-layouts  4.2 us (6%)
  other arithmetic  3.78 us (5%)
    pallas_call x1, Pallas kernels, solve_separators(): pl.pallas_call(functools.partial(kernel, (levels, n_row, rows, cols), [le...  59.3 us
    unnamed x11, local copies, waits for them, and re-layouts  2.79 us
    dot_general x1, matrix products, dot(): return jnp.dot(a, b, preferred_element_type=jnp.float32)  2.64 us
    dot_general x1, matrix products, tdot(): lax.dot_general(a, b, (((0,), (0,)), ((), ())), preferred_element_type=jn...  2.14 us
    dot_general x1, matrix products, body(): jnp.einsum('kba,kbr->kar', leaf_inv, leaf_vb.reshape(supers, block_width,...  1.81 us
    mul x1, other arithmetic, body(): coupling.reshape(supers, block_width, levels_here, sep_rows)  1.66 us

profile of v1, /device:TPU:0, one launch (start us, length us, event | category | flops | bytes accessed | tf_op | source)
XLA Modules:
  0.0 75.0 jit_solution(16241126724374310328)
XLA Ops:
  0.6 0.0 copy-start
  0.6 0.8 %convert_element_type.10 = bf16[8,3]{0,1:T(4,128)(2,1)S(1)} convert(s32[8,3]{0,1:T(4,128)} %param.9) | non-fusion elementwise | flops 24 | bytes 144 | tf_op jit(solution)/shard_map/convert_element_type | solution.py:287
  1.4 1.4 %mul.24 = bf16[8,128,3,256]{1,0,3,2:T(8,128)(2,1)} broadcast(bf16[8,3]{0,1:T(4,128)(2,1)S(1)} %convert_element_type.10), dimensions={0,2} | broadcast | bytes 1572912 | tf_op jit(solution)/shard_map/mul | solution.py:286
  2.8 1.7 %copy.9 = bf16[1024,3,256]{0,2,1:T(8,128)(2,1)S(1)} copy(bf16[1024,3,256]{2,0,1:T(8,128)(2,1)} %param.8) | data formatting | bytes 3145728 | tf_op args[2]
  4.6 0.0 copy-start.2
  4.6 1.7 %bitcast_multiply_fusion = bf16[1024,768]{0,1:T(8,128)(2,1)S(1)} fusion(bf16[96,8,8,128]{3,2,1,0:T(8,128)(2,1)} %bitcast.46, bf16[1024,3,256]{0,2,1:T(8,128)(2,1)S(1)} %copy.9), kind=kLoop, calls=%fused_computation.2 | loop fusion | flops 786432 | bytes 4718592 | tf_op jit(solution)/shard_map/mul | solution.py:286
  6.2 0.0 copy-done
  6.2 0.0 copy-done.2
  6.2 0.0 copy-start.3
  6.3 0.4 fusion.3
  6.7 1.0 %copy-done.3 = f32[1,3,256,512]{3,2,1,0:T(8,128)S(1)} copy-done((f32[1,3,256,512]{3,2,1,0:T(8,128)S(1)}, f32[1,3,256,512]{3,2,1,0:T(8,128)}, u32[]{:S(2)}) %copy-start.3) | copy-done | bytes 1572888
  7.7 2.1 %bitcast_subtract_fusion.1.share = f32[3,256,512]{2,1,0:T(8,128)} fusion(f32[1,3,256,512]{3,2,1,0:T(8,128)S(1)} %copy-done.3, bf16[3,256,1024]{2,1,0:T(8,128)(2,1)S(1)} %bitcast.49, bf16[1024,512,1]{1,0,2:T(8,128)(2,1)S(1)} %bitcast.50), kind=kOutput, calls=%fused_computation.3 | convolution fusion | flops 805699584 | bytes 5767168 | tf_op jit(solution)/shard_map/dot_general | solution.py:29
  9.8 59.3 %separators.1 = bf16[3,256,512]{2,1,0:T(8,128)(2,1)} custom-call(f32[3,256,512]{2,1,0:T(8,128)} %bitcast_subtract_fusion.1.share, bf16[6,256,1024]{2,1,0:T(8,128)(2,1)} %bitcast.47), custom_call_target="tpu_custom_call" | custom-call | tf_op jit(solution)/shard_map/separators/pallas_call | solution.py:260
  69.1 0.1 broadcast_bitcast_fusion
  69.2 2.6 %fusion = bf16[1024,512]{1,0:T(8,128)(2,1)S(1)} fusion(f32[8,128,512]{2,1,0:T(8,128)S(1)} %get-tuple-element.3, bf16[3,256,512]{2,1,0:T(8,128)(2,1)} %separators.1, bf16[1024,3,256]{2,0,1:T(8,128)(2,1)} %param.8, bf16[1024,3]{0,1:T(4,128)(2,1)S(1)} %bitcast.52), kind=kOutput, calls=%fused_computation.1 | convolution fusion | flops 807141376 | bytes 5511168 | tf_op jit(solution)/shard_map/dot_general | solution.py:33
  71.9 0.0 copy-start.1
  71.9 1.8 %fusion.4 = f32[8,512,128]{1,2,0:T(8,128)} fusion(bf16[8,128,512]{2,1,0:T(8,128)(2,1)S(1)} %bitcast.51, bf16[8,128,128]{2,1,0:T(8,128)(2,1)S(1)} %copy-done.2), kind=kOutput, calls=%fused_computation.10 | convolution fusion | flops 134217728 | bytes 3407872 | tf_op jit(solution)/shard_map/kba,kbr->kar/dot_general | solution.py:297
  73.7 0.0 copy-done.1
  73.7 1.4 %bitcast_convert_fusion = f32[1,3,256,512]{3,2,1,0:T(8,128)} fusion(bf16[3,256,512]{2,1,0:T(8,128)(2,1)S(1)} %copy-done.1), kind=kLoop, calls=%fused_computation.5 | loop fusion | flops 393216 | bytes 2359296 | tf_op jit(solution)/shard_map/broadcast_in_dim | solution.py:303
  (1 shorter events, 0.0 us)
Async XLA Ops:
  0.6 5.6 %copy-start = (bf16[1024,512]{1,0:T(8,128)(2,1)S(1)}, bf16[1024,512]{1,0:T(8,128)(2,1)}, u32[]{:S(2)}) copy-start(bf16[1024,512]{1,0:T(8,128)(2,1)} %param.6) | copy-start | bytes 3145732
  4.6 1.7 %copy-start.2 = (bf16[8,128,128]{2,1,0:T(8,128)(2,1)S(1)}, bf16[8,128,128]{2,1,0:T(8,128)(2,1)}, u32[]{:S(2)}) copy-start(bf16[8,128,128]{2,1,0:T(8,128)(2,1)} %param.7) | copy-start | bytes 786436
  6.2 1.4 %copy-start.3 = (f32[1,3,256,512]{3,2,1,0:T(8,128)S(1)}, f32[1,3,256,512]{3,2,1,0:T(8,128)}, u32[]{:S(2)}) copy-start(f32[1,3,256,512]{3,2,1,0:T(8,128)} %param.10) | copy-start | bytes 4718596
  71.9 1.8 %copy-start.1 = (bf16[3,256,512]{2,1,0:T(8,128)(2,1)S(1)}, bf16[3,256,512]{2,1,0:T(8,128)(2,1)}, u32[]{:S(2)}) copy-start(bf16[3,256,512]{2,1,0:T(8,128)(2,1)} %separators.1) | copy-start | bytes 2359300

commit v2 on v0

v2 whole, which is shorter than its diff:
```python
import functools

import jax
import jax.numpy as jnp
from jax import lax
from jax.experimental import pallas as pl
from jax.experimental.pallas import tpu as pltpu
from jax.sharding import PartitionSpec as P

MESH = pl.DeviceIdType.MESH
LANES = 128
BF, F32 = jnp.bfloat16, jnp.float32


def block_start(tree_level, level_total):
    return tree_level * level_total - tree_level * (tree_level - 1) // 2


def plan(levels, cols):
    counts, splits, count = [], [], cols // LANES
    for _ in range(levels):
        split = count % 2 == 0
        count = count // 2 if split else count
        counts.append(count)
        splits.append(split)
    return counts, splits


def tdot(a, b):
    return lax.dot_general(a, b, (((0,), (0,)), ((), ())), preferred_element_type=F32)


def dot(a, b):
    return jnp.dot(a, b, preferred_element_type=F32)


class Copies:
    def __init__(self, send, recv):
        self.send, self.recv, self.count, self.all = send, recv, 0, []

    def start(self, src, dst, device):
        copy = pltpu.make_async_remote_copy(
            src_ref=src,
            dst_ref=dst,
            send_sem=self.send.at[self.count],
            recv_sem=self.recv.at[self.count],
            device_id=device,
            device_id_type=MESH,
        )
        copy.start()
        self.count += 1
        self.all.append(copy)
        return copy


def copies_needed(levels, n_row, counts, splits):
    half = n_row // 2
    total = 0
    for t in range(levels):
        each = 2 + 1 + 2 * (half - 1) + half + half - 1
        each += (levels - t) if splits[t] else 0
        total += each * counts[t]
    return total


def kernel(dims, rhs_in, inv_in, coup_in, pat, ancr_in, anc_in, leaf_out, out, *scratch):
    levels, n_row, blocks, supers, width = dims
    rhs, inv, coup, ancr, anc, ly, yb, mk, mt, atr, pend, wide = scratch[:12]
    used = 12
    groups = []
    for _ in range(8):
        groups.append(scratch[used : used + levels])
        used += levels
    tx, rx, zs, acc, ps, pr, qs, qr = groups
    send, recv, local = scratch[used:]
    counts, splits = plan(levels, blocks * LANES)
    rows = anc.shape[1]
    half = n_row // 2
    lay = lax.axis_index("layer")
    row = lax.axis_index("row")
    core = lax.rem(row, 2)
    yy = row // 2
    mate = {"row": yy * 2 + (1 - core)}
    bits = [lax.rem(lay // 2**t, 2) for t in range(levels)]
    across = [{"layer": lay + (1 - 2 * bits[t]) * 2**t} for t in range(levels)]

    loads = []
    for n, (src, dst) in enumerate(
        [(rhs_in, rhs), (inv_in, inv)]
        + [(coup_in.at[s], coup.at[s]) for s in range(levels)]
        + [(ancr_in, ancr), (anc_in, anc)]
    ):
        load = pltpu.make_async_copy(src, dst, local.at[n])
        load.start()
        loads.append(load)

    barrier = pltpu.get_barrier_semaphore()
    for t in range(levels):
        pl.semaphore_signal(barrier, inc=1, device_id=across[t], device_id_type=MESH)
    for i in range(1, n_row):
        pl.semaphore_signal(
            barrier, inc=1, device_id={"row": lax.rem(row + i, n_row)}, device_id_type=MESH
        )
    copies = Copies(send, recv)

    order = list(range(counts[-1]))
    for t in reversed(range(levels)):
        if splits[t]:
            near = [bits[t] * counts[t] + j for j in order]
            order = [(1 - bits[t]) * counts[t] + j for j in order] + near
    columns = [pl.ds(pl.multiple_of(j * LANES, LANES), LANES) for j in order]

    def own(t):
        return list(range(blocks - counts[t], blocks))

    def theirs(t, p):
        return p - counts[t] if splits[t] else p

    loads[0].wait()
    loads[1].wait()
    for k in range(supers):
        part = slice(k * width, (k + 1) * width)
        value = dot(inv[k], rhs[part])
        ly[part] = value
        yb[part] = value.astype(BF)

    def mask(s):
        loads[2 + s].wait()
        cut = slice(s * rows, (s + 1) * rows)
        for k in range(supers):
            part = slice(k * width, (k + 1) * width)
            value = coup[s, part].astype(F32) * pat[k, s].astype(F32)
            mk[part, cut] = value.astype(BF)
            mt[s, :, part] = value.T.astype(BF)

    def share(s, where):
        for first in range(0, len(where), 2):
            two = where[first : first + 2]
            value = dot(mt[s], jnp.concatenate([yb[:, columns[p]] for p in two], axis=1))
            for n, p in enumerate(two):
                yield ancr[s, :, columns[p]] - value[:, n * LANES : (n + 1) * LANES]

    flight = {}

    def offer_urgent(t, p, value):
        n = p - (blocks - counts[t])
        tx[t][n, 0] = value.astype(BF)
        one = pl.ds(0, 1)
        flight[t, p, 0] = copies.start(tx[t].at[n, one], rx[t].at[n, one], across[t])

    def offer_rest(t, p, values):
        if t + 1 == levels:
            return
        n = p - (blocks - counts[t])
        for k, value in enumerate(values):
            tx[t][n, 1 + k] = value.astype(BF)
        later = pl.ds(1, levels - t - 1)
        flight[t, p, 1] = copies.start(tx[t].at[n, later], rx[t].at[n, later], across[t])

    mask(0)
    loads[2 + levels].wait()
    mine = own(0)
    away = [theirs(0, p) for p in mine]
    first_shares = list(share(0, away))
    pl.semaphore_wait(barrier, levels + n_row - 1)
    for p, value in zip(mine, first_shares):
        offer_urgent(0, p, value)
    for p, value in zip(mine, share(0, mine)):
        pend[0, p] = value
    for s in range(1, levels):
        mask(s)
    later_shares = [list(share(s, away)) for s in range(1, levels)]
    for n, p in enumerate(mine):
        offer_rest(0, p, [values[n] for values in later_shares])
    for s in range(1, levels):
        for p, value in zip(mine, share(s, mine)):
            pend[s, p] = value
    loads[3 + levels].wait()

    def turn(k):
        for other in range(n_row):
            cut = slice(other * rows, (other + 1) * rows)
            atr[k, cut] = anc[k, :, cut].T

    later_work = None
    for t in range(levels):
        first_block = block_start(t, levels)
        above = levels - t - 1
        if later_work is not None:
            later_work()
        gathers, to_mate = {}, {}
        for p in own(t):
            n = p - (blocks - counts[t])
            flight[t, p, 0].wait_recv()
            zs[t][n, row] = (pend[t, p] + rx[t][n, 0].astype(F32)).astype(BF)
            spot = zs[t].at[n, row]
            for i in range(1, half):
                other = lax.rem(yy + i, half) * 2 + core
                gathers[p, i] = copies.start(spot, spot, {"row": other})
            to_mate[p] = copies.start(spot, spot, mate)
        for s in range(t + 1, levels):
            turn(first_block + s - t)
        for p in own(t):
            n = p - (blocks - counts[t])

            def sums_of(slot, n=n):
                cut = pl.ds(pl.multiple_of(slot * rows, LANES), rows)
                return [dot(anc[first_block + 1 + k, :, cut], zs[t][n, slot]) for k in range(above)]

            def add(old, new):
                return [a + b for a, b in zip(old, new)]

            total = sums_of(row)
            to_mate[p].wait_recv()
            total = add(total, sums_of(yy * 2 + 1 - core))
            passed = {}
            for i in range(1, half):
                gathers[p, i].wait_recv()
                origin = lax.rem(yy - i + half, half) * 2
                spot = zs[t].at[n, origin + core]
                passed[i] = copies.start(spot, spot, mate)
                total = add(total, sums_of(origin + core))
            for i in range(1, half):
                passed[i].wait_recv()
                origin = lax.rem(yy - i + half, half) * 2
                total = add(total, sums_of(origin + 1 - core))
            if above:
                flight[t, p, 1].wait_recv()
            for k in range(above):
                pend[t + 1 + k, p] = pend[t + 1 + k, p] + rx[t][n, 1 + k].astype(F32) - total[k]
            if above:
                for q in own(t + 1):
                    if theirs(t + 1, q) == p:
                        offer_urgent(t + 1, q, pend[t + 1, p])
                        offer_rest(t + 1, q, [pend[s, p] for s in range(t + 2, levels)])

        def later_work(t=t, first_block=first_block):
            z_all = jnp.concatenate(
                [zs[t][n].reshape(n_row * rows, LANES) for n in range(counts[t])], axis=1
            )
            y_here = dot(anc[first_block], z_all).astype(BF)
            for other in range(n_row):
                acc[t][other] = tdot(anc[first_block, :, other * rows : (other + 1) * rows], y_here)

    later_work()

    arriving = {}

    def need(s, p):
        copy = arriving.pop((s, p), None)
        if copy is not None:
            copy.wait_recv()

    def widen(s, p, t):
        if splits[t]:
            arriving[s, p - counts[t]] = copies.start(
                wide.at[s, p], wide.at[s, p - counts[t]], across[t]
            )

    def leaf_back(first, last, p):
        terms = jnp.concatenate([wide[s, p] for s in range(first, last)], axis=0)
        return ly[:, columns[p]] - dot(mk[:, first * rows : last * rows], terms)

    ring = list(range(1, half)) + [0]
    for t in reversed(range(levels)):
        first_block = block_start(t, levels)
        second, kept = {}, {}
        for p in reversed(own(t)):
            n = p - (blocks - counts[t])
            for s in range(t + 1, levels):
                need(s, p)

            def part_of(dest, p=p, n=n):
                value = acc[t][dest, :, n * LANES : (n + 1) * LANES]
                cut = pl.ds(pl.multiple_of(dest * rows, LANES), rows)
                for s in range(t + 1, levels):
                    value = value - dot(atr[first_block + s - t, cut], wide[s, p])
                return value

            first = {}
            for i in ring:
                dest = lax.rem(yy + i, half) * 2 + 1 - core
                ps[t][n, i] = part_of(dest).astype(BF)
                first[i] = copies.start(ps[t].at[n, i], pr[t].at[n, i], mate)
            for s in range(t + 1, levels):
                widen(s, p, t)
            for i in ring[:-1]:
                dest = lax.rem(yy + i, half) * 2 + core
                value = part_of(dest)
                first[i].wait_recv()
                qs[t][n, i - 1] = (value + pr[t][n, i].astype(F32)).astype(BF)
                second[p, i] = copies.start(
                    qs[t].at[n, i - 1], qr[t].at[n, i - 1], {"row": dest}
                )
            value = part_of(row)
            first[0].wait_recv()
            kept[p] = value + pr[t][n, 0].astype(F32)
            if t == 0 and levels > 1:
                ly[:, columns[p]] = leaf_back(1, levels, p)
        for p in reversed(own(t)):
            n = p - (blocks - counts[t])
            value = kept[p]
            for i in ring[:-1]:
                second[p, i].wait_recv()
                value = value + qr[t][n, i - 1].astype(F32)
            wide[t, p] = value.astype(BF)
            widen(t, p, t)
    for p in reversed(own(0)):
        leaf_out[:, columns[p]] = leaf_back(0, 1, p).astype(BF)
    for p in reversed(range(blocks - counts[0])):
        for s in range(1, levels):
            need(s, p)
        if levels > 1:
            ly[:, columns[p]] = leaf_back(1, levels, p)
    for s in range(levels):
        for p in own(0):
            out[s, :, columns[p]] = wide[s, p]
    for p in reversed(range(blocks - counts[0])):
        need(0, p)
        leaf_out[:, columns[p]] = leaf_back(0, 1, p).astype(BF)
        for s in range(levels):
            out[s, :, columns[p]] = wide[s, p]
    for copy in copies.all:
        copy.wait_send()


def solve(leaf_rhs, leaf_inv, coupling, pattern, anc_rhs, anc):
    levels, rows, cols = anc_rhs.shape
    leaf_rows = leaf_rhs.shape[0]
    supers, width = leaf_inv.shape[:2]
    n_row = lax.axis_size("row")
    half = n_row // 2
    blocks = cols // LANES
    counts, splits = plan(levels, cols)
    span = range(levels)
    less = max(half - 1, 1)
    scratch = [
        pltpu.VMEM(leaf_rhs.shape, BF),
        pltpu.VMEM(leaf_inv.shape, BF),
        pltpu.VMEM(coupling.shape, BF),
        pltpu.VMEM(anc_rhs.shape, F32),
        pltpu.VMEM(anc.shape, BF),
        pltpu.VMEM((leaf_rows, cols), F32),
        pltpu.VMEM((leaf_rows, cols), BF),
        pltpu.VMEM((leaf_rows, levels * rows), BF),
        pltpu.VMEM((levels, rows, leaf_rows), BF),
        pltpu.VMEM((anc.shape[0], n_row * rows, rows), BF),
        pltpu.VMEM((levels, blocks, rows, LANES), F32),
        pltpu.VMEM((levels, blocks, rows, LANES), BF),
    ]
    scratch += [pltpu.VMEM((counts[t], levels - t, rows, LANES), BF) for t in span]
    scratch += [pltpu.VMEM((counts[t], levels - t, rows, LANES), BF) for t in span]
    scratch += [pltpu.VMEM((counts[t], n_row, rows, LANES), BF) for t in span]
    scratch += [pltpu.VMEM((n_row, rows, counts[t] * LANES), F32) for t in span]
    scratch += [pltpu.VMEM((counts[t], half, rows, LANES), BF) for t in span]
    scratch += [pltpu.VMEM((counts[t], half, rows, LANES), BF) for t in span]
    scratch += [pltpu.VMEM((counts[t], less, rows, LANES), BF) for t in span]
    scratch += [pltpu.VMEM((counts[t], less, rows, LANES), BF) for t in span]
    total = copies_needed(levels, n_row, counts, splits)
    scratch += [pltpu.SemaphoreType.DMA((total,)), pltpu.SemaphoreType.DMA((total,))]
    scratch += [pltpu.SemaphoreType.DMA((levels + 4,))]
    away = pl.BlockSpec(memory_space=pl.ANY)
    return pl.pallas_call(
        functools.partial(kernel, (levels, n_row, blocks, supers, width)),
        out_shape=(
            jax.ShapeDtypeStruct((leaf_rows, cols), BF),
            jax.ShapeDtypeStruct((levels, rows, cols), BF),
        ),
        in_specs=[away, away, away, pl.BlockSpec(memory_space=pltpu.SMEM), away, away],
        out_specs=(pl.BlockSpec(memory_space=pltpu.VMEM),) * 2,
        scratch_shapes=scratch,
        compiler_params=pltpu.CompilerParams(collective_id=0, has_side_effects=True),
        name="solve",
    )(leaf_rhs, leaf_inv, coupling, pattern, anc_rhs, anc)


def body(leaf_rhs, leaf_inv, coupling, pattern, anc_rhs, anc_blocks):
    supers, width = leaf_inv.shape[:2]
    leaf_rows, cols = leaf_rhs.shape
    leaf_vb, solved = solve(
        leaf_rhs, leaf_inv, coupling.transpose(1, 0, 2), pattern, anc_rhs[0], anc_blocks[0]
    )
    x_leaf = jnp.einsum(
        "kba,kbr->kar",
        leaf_inv,
        leaf_vb.reshape(supers, width, cols),
        preferred_element_type=F32,
    )
    return (x_leaf.reshape(leaf_rows, cols), solved.astype(F32)[None])


def solution(mesh):
    placed = (
        P(("layer", "row"), None),
        P(("layer", "row"), None, None),
        P(("layer", "row"), None, None),
        P(("layer", "row"), None),
        P("layer", None, "row", None),
        P("layer", None, "row", None),
    )
    return jax.shard_map(
        body,
        mesh=mesh,
        in_specs=placed,
        out_specs=(P(("layer", "row"), None), P("layer", None, "row", None)),
        check_vma=False,
    )
```

time: 285 us -> 62.6 us (0.22)
  waiting for transfers between devices: 223 us -> 0 us
  Pallas kernels: 0 us -> 55.9 us
  matrix products: 22.9 us -> 3.1 us
  between operations: 14.3 us -> 0.66 us
  local copies, waits for them, and re-layouts: 9.83 us -> 1.36 us
  starting transfers between devices: 7.23 us -> 0 us
  other arithmetic: 7.43 us -> 1.35 us
    reduce_scatter x3 -> x0, waiting for transfers between devices: 91.6 us -> none  [body(): lax.psum_scatter(transposed(jnp.int32(0), sep_rows * lax.axis_size('row')...]
    ppermute x3 -> x0, waiting for transfers between devices: 82 us -> none  [partner(): return lax.ppermute(value, axis, pairs)]
    pallas_call x0 -> x1, Pallas kernels: none -> 55.9 us  [solve(): pl.pallas_call(functools.partial(kernel, (levels, n_row, blocks, supers,...]
    all_gather x3 -> x0, waiting for transfers between devices: 49.2 us -> none  [body(): lax.all_gather(level_z, 'row', axis=0, tiled=True)]
    dot_general x9 -> x1, matrix products: 22.9 us -> 3.1 us  [body(): jnp.einsum('kba,kbr->kar', leaf_inv, leaf_vb.reshape(supers, width, cols)...]
    ppermute x3 -> x0, starting transfers between devices: 6.98 us -> none  [partner(): return lax.ppermute(value, axis, pairs)]
    slice x5 -> x0, local copies, waits for them, and re-layouts: 4.15 us -> none  [the longest x3 2.68 us: body(): factor = anc_blocks[0, first_block:first_block + block_count]]
  transfers between devices with their start and end apart: 9 -> 0, of which waited for: 9 -> 0; matrix products, arithmetic and copies ran while one was open for 2% -> 0% of each run, Pallas kernels for 0% -> 0%
where the time goes in v2:
time: 62.6 us; the launch traced here: 62.4 us
  Pallas kernels  55.9 us (89%)
  matrix products  3.1 us (5%)
  local copies, waits for them, and re-layouts  1.36 us (2%)
  other arithmetic  1.35 us (2%)
  between operations  0.66 us (1%)
    pallas_call x1, Pallas kernels, solve(): pl.pallas_call(functools.partial(kernel, (levels, n_row, blocks, supers,...  55.9 us
    dot_general x1, matrix products, body(): jnp.einsum('kba,kbr->kar', leaf_inv, leaf_vb.reshape(supers, width, cols)...  3.1 us
    unnamed x5, local copies, waits for them, and re-layouts  1.36 us
    broadcast_in_dim x1, other arithmetic, body(): return (x_leaf.reshape(leaf_rows, cols), solved.astype(F32)[None])  1.35 us

profile of v2, /device:TPU:0, one launch (start us, length us, event | category | flops | bytes accessed | tf_op | source)
XLA Modules:
  0.0 62.4 jit_solution(8064445912325084072)
XLA Ops:
  0.6 1.3 %copy.8.pat = s32[8,3]{1,0:T(8,128)} copy(s32[8,3]{0,1:T(4,128)} %param.9) | data formatting | bytes 192 | tf_op args[3]
  2.0 0.0 copy-start
  2.0 55.9 %solve.1 = (bf16[1024,512]{1,0:T(8,128)(2,1)}, bf16[3,256,512]{2,1,0:T(8,128)(2,1)}) custom-call(bf16[1024,512]{1,0:T(8,128)(2,1)} %rhs_in.1, bf16[8,128,128]{2,1,0:T(8,128)(2,1)} %inv_in.1, bf16[3,1024,256]{2,1,0:T(8,128)(2,1)} %bitcast.14, s32[8,3]{1,0:T(8,128)} %copy.8.pat, f32[3,256,512]{2,1,0:T(8,128)} %bitcast.15, bf16[6,256,1024]{2,1,0:T(8,128)(2,1)} %bitcast.12), custom_call_target="tpu_custom_call" | custom-call | tf_op jit(solution)/shard_map/solve/pallas_call | solution.py:363
  57.9 0.0 copy-done
  57.9 0.0 copy-start.1
  57.9 3.1 %fusion = f32[8,512,128]{1,2,0:T(8,128)} fusion(bf16[8,128,512]{2,1,0:T(8,128)(2,1)} %bitcast.16, bf16[8,128,128]{2,1,0:T(8,128)(2,1)S(1)} %copy-done), kind=kOutput, calls=%fused_computation.1 | convolution fusion | flops 134217728 | bytes 3407872 | tf_op jit(solution)/shard_map/kba,kbr->kar/dot_general | solution.py:383
  61.0 0.0 copy-done.1
  61.0 1.4 %bitcast_convert_fusion = f32[1,3,256,512]{3,2,1,0:T(8,128)} fusion(bf16[3,256,512]{2,1,0:T(8,128)(2,1)S(1)} %copy-done.1), kind=kLoop, calls=%fused_computation | loop fusion | flops 393216 | bytes 2359296 | tf_op jit(solution)/shard_map/broadcast_in_dim | solution.py:389
Async XLA Ops:
  2.0 55.9 %copy-start = (bf16[8,128,128]{2,1,0:T(8,128)(2,1)S(1)}, bf16[8,128,128]{2,1,0:T(8,128)(2,1)}, u32[]{:S(2)}) copy-start(bf16[8,128,128]{2,1,0:T(8,128)(2,1)} %inv_in.1) | copy-start | bytes 786436
  57.9 3.1 %copy-start.1 = (bf16[3,256,512]{2,1,0:T(8,128)(2,1)S(1)}, bf16[3,256,512]{2,1,0:T(8,128)(2,1)}, u32[]{:S(2)}) copy-start(bf16[3,256,512]{2,1,0:T(8,128)(2,1)} %get-tuple-element.5) | copy-start | bytes 2359300

commit v3 on v2

--- a/solution.py
+++ b/solution.py
@@ -129,7 +129,7 @@
         cut = slice(s * rows, (s + 1) * rows)
         for k in range(supers):
             part = slice(k * width, (k + 1) * width)
-            value = coup[s, part].astype(F32) * pat[k, s].astype(F32)
+            value = coup[s, part].astype(F32) * pat[s, k].astype(F32)
             mk[part, cut] = value.astype(BF)
             mt[s, :, part] = value.T.astype(BF)
 
@@ -182,7 +182,7 @@
             cut = slice(other * rows, (other + 1) * rows)
             atr[k, cut] = anc[k, :, cut].T
 
-    later_work = None
+    later_work, top_y = None, {}
     for t in range(levels):
         first_block = block_start(t, levels)
         above = levels - t - 1
@@ -200,12 +200,17 @@
             to_mate[p] = copies.start(spot, spot, mate)
         for s in range(t + 1, levels):
             turn(first_block + s - t)
+        if not above:
+            turn(first_block)
+        skip = 1 if above else 0
         for p in own(t):
             n = p - (blocks - counts[t])
 
             def sums_of(slot, n=n):
                 cut = pl.ds(pl.multiple_of(slot * rows, LANES), rows)
-                return [dot(anc[first_block + 1 + k, :, cut], zs[t][n, slot]) for k in range(above)]
+                return [
+                    dot(anc[first_block + k, :, cut], zs[t][n, slot]) for k in range(skip, above + 1)
+                ]
 
             def add(old, new):
                 return [a + b for a, b in zip(old, new)]
@@ -226,6 +231,8 @@
                 total = add(total, sums_of(origin + 1 - core))
             if above:
                 flight[t, p, 1].wait_recv()
+            else:
+                top_y[p] = total[0].astype(BF)
             for k in range(above):
                 pend[t + 1 + k, p] = pend[t + 1 + k, p] + rx[t][n, 1 + k].astype(F32) - total[k]
             if above:
@@ -241,8 +248,6 @@
             y_here = dot(anc[first_block], z_all).astype(BF)
             for other in range(n_row):
                 acc[t][other] = tdot(anc[first_block, :, other * rows : (other + 1) * rows], y_here)
-
-    later_work()
 
     arriving = {}
 
@@ -271,8 +276,10 @@
                 need(s, p)
 
             def part_of(dest, p=p, n=n):
+                cut = pl.ds(pl.multiple_of(dest * rows, LANES), rows)
+                if t + 1 == levels:
+                    return dot(atr[first_block, cut], top_y[p])
                 value = acc[t][dest, :, n * LANES : (n + 1) * LANES]
-                cut = pl.ds(pl.multiple_of(dest * rows, LANES), rows)
                 for s in range(t + 1, levels):
                     value = value - dot(atr[first_block + s - t, cut], wide[s, p])
                 return value
@@ -295,7 +302,7 @@
             value = part_of(row)
             first[0].wait_recv()
             kept[p] = value + pr[t][n, 0].astype(F32)
-            if t == 0 and levels > 1:
+            if t == 0 and levels > 1 and p != own(t)[0]:
                 ly[:, columns[p]] = leaf_back(1, levels, p)
         for p in reversed(own(t)):
             n = p - (blocks - counts[t])
@@ -305,6 +312,8 @@
                 value = value + qr[t][n, i - 1].astype(F32)
             wide[t, p] = value.astype(BF)
             widen(t, p, t)
+            if t == 0 and levels > 1 and p == own(t)[-1]:
+                ly[:, columns[own(t)[0]]] = leaf_back(1, levels, own(t)[0])
     for p in reversed(own(0)):
         leaf_out[:, columns[p]] = leaf_back(0, 1, p).astype(BF)
     for p in reversed(range(blocks - counts[0])):
@@ -374,19 +383,41 @@
     )(leaf_rhs, leaf_inv, coupling, pattern, anc_rhs, anc)
 
 
+def tail_kernel(inv, vb, solved, x_leaf, x_anc):
+    count, width = inv.shape[:2]
+    for k in range(count):
+        part = slice(k * width, (k + 1) * width)
+        x_leaf[part] = tdot(inv[k], vb[part])
+    x_anc[...] = solved[...].astype(F32)
+
+
+def tail(leaf_inv, leaf_vb, solved):
+    supers, width = leaf_inv.shape[:2]
+    leaf_rows, cols = leaf_vb.shape
+    anc_rows = solved.shape[0]
+    steps = 4 if supers % 4 == 0 and anc_rows % 64 == 0 else 1
+    rows = [leaf_rows // steps, anc_rows // steps]
+    flat = [pl.BlockSpec((n, cols), lambda i: (i, 0)) for n in rows]
+    return pl.pallas_call(
+        tail_kernel,
+        grid=(steps,),
+        out_shape=(
+            jax.ShapeDtypeStruct((leaf_rows, cols), F32),
+            jax.ShapeDtypeStruct((anc_rows, cols), F32),
+        ),
+        in_specs=[pl.BlockSpec((supers // steps, width, width), lambda i: (i, 0, 0))] + flat,
+        out_specs=tuple(flat),
+        name="tail",
+    )(leaf_inv, leaf_vb, solved)
+
+
 def body(leaf_rhs, leaf_inv, coupling, pattern, anc_rhs, anc_blocks):
-    supers, width = leaf_inv.shape[:2]
-    leaf_rows, cols = leaf_rhs.shape
+    _, levels, rows, cols = anc_rhs.shape
     leaf_vb, solved = solve(
-        leaf_rhs, leaf_inv, coupling.transpose(1, 0, 2), pattern, anc_rhs[0], anc_blocks[0]
+        leaf_rhs, leaf_inv, coupling.transpose(1, 0, 2), pattern.T, anc_rhs[0], anc_blocks[0]
     )
-    x_leaf = jnp.einsum(
-        "kba,kbr->kar",
-        leaf_inv,
-        leaf_vb.reshape(supers, width, cols),
-        preferred_element_type=F32,
-    )
-    return (x_leaf.reshape(leaf_rows, cols), solved.astype(F32)[None])
+    x_leaf, x_anc = tail(leaf_inv, leaf_vb, solved.reshape(levels * rows, cols))
+    return (x_leaf, x_anc.reshape(1, levels, rows, cols))
 
 
 def solution(mesh):

time: 62.6 us -> 60.9 us (0.973)
  Pallas kernels: 55.9 us -> 60.1 us
  matrix products: 3.1 us -> 0 us
  local copies, waits for them, and re-layouts: 1.36 us -> 0 us
  other arithmetic: 1.35 us -> 0 us
    pallas_call x0 -> x1, Pallas kernels: none -> 4.32 us  [tail(): pl.pallas_call(tail_kernel, grid=(steps,), out_shape=(jax.ShapeDtypeStruc...]
    dot_general x1 -> x0, matrix products: 3.1 us -> none  [body(): jnp.einsum('kba,kbr->kar', leaf_inv, leaf_vb.reshape(supers, width, cols)...]
    unnamed x5 -> x0, local copies, waits for them, and re-layouts: 1.36 us -> none
    broadcast_in_dim x1 -> x0, other arithmetic: 1.35 us -> none  [body(): return (x_leaf.reshape(leaf_rows, cols), solved.astype(F32)[None])]
where the time goes in v3:
time: 60.9 us; the launch traced here: 60.7 us
  Pallas kernels  60.1 us (99%)
  between operations  0.64 us (1%)
    pallas_call x1, Pallas kernels, solve(): pl.pallas_call(functools.partial(kernel, (levels, n_row, blocks, supers,...  55.8 us
    pallas_call x1, Pallas kernels, tail(): pl.pallas_call(tail_kernel, grid=(steps,), out_shape=(jax.ShapeDtypeStruc...  4.32 us

profile of v3, /device:TPU:0, one launch (start us, length us, event | category | flops | bytes accessed | tf_op | source)
XLA Modules:
  0.0 60.7 jit_solution(15500087136769680981)
XLA Ops:
  0.6 55.8 %solve.1 = (bf16[1024,512]{1,0:T(8,128)(2,1)}, bf16[3,256,512]{2,1,0:T(8,128)(2,1)}) custom-call(bf16[1024,512]{1,0:T(8,128)(2,1)} %rhs_in.1, bf16[8,128,128]{2,1,0:T(8,128)(2,1)} %inv.1, bf16[3,1024,256]{2,1,0:T(8,128)(2,1)} %bitcast.7, s32[3,8]{1,0:T(4,128)} %bitcast.10, f32[3,256,512]{2,1,0:T(8,128)} %bitcast.8, bf16[6,256,1024]{2,1,0:T(8,128)(2,1)} %bitcast.6), custom_call_target="tpu_custom_call" | custom-call | tf_op jit(solution)/shard_map/solve/pallas_call | solution.py:372
  56.4 4.3 %tail.1 = (f32[1024,512]{1,0:T(8,128)}, f32[768,512]{1,0:T(8,128)}) custom-call(bf16[8,128,128]{2,1,0:T(8,128)(2,1)} %inv.1, bf16[1024,512]{1,0:T(8,128)(2,1)} %get-tuple-element.6.vb, bf16[768,512]{1,0:T(8,128)(2,1)} %bitcast.9), custom_call_target="tpu_custom_call" | custom-call | tf_op jit(solution)/shard_map/tail/pallas_call | solution.py:401

commit v4 on v3

--- a/solution.py
+++ b/solution.py
@@ -395,7 +395,7 @@
     supers, width = leaf_inv.shape[:2]
     leaf_rows, cols = leaf_vb.shape
     anc_rows = solved.shape[0]
-    steps = 4 if supers % 4 == 0 and anc_rows % 64 == 0 else 1
+    steps = 2 if supers % 2 == 0 and anc_rows % 32 == 0 else 1
     rows = [leaf_rows // steps, anc_rows // steps]
     flat = [pl.BlockSpec((n, cols), lambda i: (i, 0)) for n in rows]
     return pl.pallas_call(

time: 60.9 us -> 59.9 us (0.984)
  Pallas kernels: 60.1 us -> 59.1 us
    pallas_call x1, Pallas kernels: 4.32 us -> 3.35 us  [tail(): pl.pallas_call(tail_kernel, grid=(steps,), out_shape=(jax.ShapeDtypeStruc...]
where the time goes in v4:
time: 59.9 us; the launch traced here: 59.8 us
  Pallas kernels  59.1 us (99%)
  between operations  0.64 us (1%)
    pallas_call x1, Pallas kernels, solve(): pl.pallas_call(functools.partial(kernel, (levels, n_row, blocks, supers,...  55.8 us
    pallas_call x1, Pallas kernels, tail(): pl.pallas_call(tail_kernel, grid=(steps,), out_shape=(jax.ShapeDtypeStruc...  3.35 us

profile of v4, /device:TPU:0, one launch (start us, length us, event | category | flops | bytes accessed | tf_op | source)
XLA Modules:
  0.0 59.8 jit_solution(13541004689331716303)
XLA Ops:
  0.6 55.8 %solve.1 = (bf16[1024,512]{1,0:T(8,128)(2,1)}, bf16[3,256,512]{2,1,0:T(8,128)(2,1)}) custom-call(bf16[1024,512]{1,0:T(8,128)(2,1)} %rhs_in.1, bf16[8,128,128]{2,1,0:T(8,128)(2,1)} %inv.1, bf16[3,1024,256]{2,1,0:T(8,128)(2,1)} %bitcast.7, s32[3,8]{1,0:T(4,128)} %bitcast.10, f32[3,256,512]{2,1,0:T(8,128)} %bitcast.8, bf16[6,256,1024]{2,1,0:T(8,128)(2,1)} %bitcast.6), custom_call_target="tpu_custom_call" | custom-call | tf_op jit(solution)/shard_map/solve/pallas_call | solution.py:372
  56.4 3.3 %tail.1 = (f32[1024,512]{1,0:T(8,128)}, f32[768,512]{1,0:T(8,128)}) custom-call(bf16[8,128,128]{2,1,0:T(8,128)(2,1)} %inv.1, bf16[1024,512]{1,0:T(8,128)(2,1)} %get-tuple-element.6.vb, bf16[768,512]{1,0:T(8,128)(2,1)} %bitcast.9), custom_call_target="tpu_custom_call" | custom-call | tf_op jit(solution)/shard_map/tail/pallas_call | solution.py:401
